TPU v7x, 32 devices: a whole 2x2x4 slice. The times are simulated.
32 devices in a mesh: ctx: 8 (over z, y), tp: 4 (over x, core).
Axes of the slice: x: 2, y: 2, z: 4, core: 2. Of those that a mesh axis runs over, the one named last changes fastest.
Arguments:
- queries: bfloat16 [1024, 8192], P('ctx', 'tp'), may hold values from -6 to 6
- keys: bfloat16 [1024, 8192], P('ctx', 'tp'), may hold values from -6 to 6
- values: bfloat16 [1024, 8192], P('ctx', 'tp'), may hold values from -6 to 6
- short_taps: float32 [3, 3, 8192], P(None, None, 'tp'), may hold values from -3.5 to 3.5
- long_rates: float32 [8192, 16], P('tp'), may hold values from 1.953125e-05 to 0.05
- long_resid: float32 [8192, 16], P('tp'), may hold values from -1.5 to 1.5
- out_weight: bfloat16 [8192, 4096], P('tp'), may hold values from -0.09375 to 0.09375
Outputs:
- block_out: bfloat16 [1024, 4096], P('ctx', 'tp')
All inputs are finite; a program needn't handle non-finite values.
Results may differ from a plain program's by a relative error of at most 0.017.
Values may be sent and summed in bfloat16 or wider, within the bound.
No kernel may reach another device: no remote copies, remote signals or barrier semaphores. Data moves between devices by JAX's collectives and lax.ppermute only.
A program may use at most 128 MiB of HBM per device.

v0:
```python
import math

import jax
import jax.numpy as jnp
from jax import lax
from jax.sharding import PartitionSpec as P


def shifted(value, axis, steps):
    count = lax.axis_size(axis)
    initial, last = (max(0, -steps), min(count, count - steps))
    return lax.ppermute(value, axis, [(source, source + steps) for source in range(initial, last)])


def causal_taps(stream, leading, filter_taps):
    tok_rows = stream.shape[0]
    tail_len = filter_taps.shape[0] - 1
    extended = jnp.concatenate([leading, stream], axis=0).astype(jnp.float32)
    accum_sum = jnp.zeros(stream.shape, jnp.float32)
    for tap_index in range(filter_taps.shape[0]):
        accum_sum = (
            accum_sum
            + filter_taps[tap_index]
            * extended[tail_len - tap_index : tail_len - tap_index + tok_rows]
        )
    return accum_sum


def by_groups(inner_fn, arrays):
    channels = arrays[0].shape[0]
    group = math.gcd(channels, 128)
    stacked = tuple((item.reshape((channels // group, group) + item.shape[1:]) for item in arrays))
    result = lax.map(lambda pieces: inner_fn(*pieces), stacked)
    return result.reshape((channels,) + result.shape[2:])


def modal_conv(signal, decay_rates, residues, state_start):
    better = lax.Precision.HIGH
    channels, length = signal.shape
    block_len = math.gcd(length, 256)
    num_blocks = length // block_len
    mode_gain = residues * jnp.sqrt(-jnp.expm1(-2.0 * decay_rates))
    positions = jnp.arange(block_len, dtype=jnp.float32)
    grow_pow = jnp.exp(-decay_rates[:, None, :] * positions[None, :, None])
    left_side = grow_pow * mode_gain[:, None, :]
    kernel = jnp.sum(left_side, axis=2)
    row_index = jnp.arange(block_len, dtype=jnp.int32)
    offset_table = row_index[:, None] - row_index[None, :]
    causal_mask = offset_table >= 0
    toeplitz = jnp.take(kernel, jnp.maximum(offset_table, 0), axis=1)
    toeplitz = jnp.where(causal_mask[None], toeplitz, 0.0)
    blocks_in = signal.reshape(channels, num_blocks, block_len)
    inner_part = jnp.einsum("cij,cbj->cbi", toeplitz, blocks_in, precision=better)
    tail_pow = jnp.exp(-decay_rates[:, None, :] * (block_len - 1.0 - positions)[None, :, None])
    block_ends = jnp.einsum("cbj,cjm->cbm", blocks_in, tail_pow, precision=better)
    block_idx = jnp.arange(num_blocks, dtype=jnp.float32)
    gap_count = block_idx[:, None] - block_idx[None, :] - 1.0
    carry_decay = jnp.exp(
        -decay_rates[:, :, None, None] * block_len * jnp.maximum(gap_count, 0.0)[None, None]
    )
    carry_decay = jnp.where((gap_count >= 0.0)[None, None], carry_decay, 0.0)
    states = jnp.einsum("cmbk,ckm->cbm", carry_decay, block_ends, precision=better)
    states = (
        states
        + jnp.exp(-decay_rates[:, None, :] * (block_len * block_idx)[None, :, None])
        * state_start[:, None, :]
    )
    after_one = left_side * jnp.exp(-decay_rates)[:, None, :]
    outer_part = jnp.einsum("cim,cbm->cbi", after_one, states, precision=better)
    return (inner_part + outer_part).reshape(channels, length)


def shards(queries, keys, values, short_taps, long_rates, long_resid, out_weight):
    tok_rows, channels = queries.shape
    tail_len = short_taps.shape[1] - 1
    leading = shifted(
        (
            queries[tok_rows - tail_len :],
            keys[tok_rows - tail_len :],
            values[tok_rows - tail_len :],
        ),
        "ctx",
        1,
    )
    q_feat = causal_taps(queries, leading[0], short_taps[0])
    k_feat = causal_taps(keys, leading[1], short_taps[1])
    v_feat = causal_taps(values, leading[2], short_taps[2])
    product = (k_feat * v_feat).astype(jnp.bfloat16)
    modes = long_rates.shape[1]
    channel_share = channels // lax.axis_size("ctx")
    turned = lax.all_to_all(product.T, "ctx", split_axis=0, concat_axis=1, tiled=True)
    first_row = lax.axis_index("ctx") * channel_share
    rate_slice = lax.dynamic_slice_in_dim(long_rates, first_row, channel_share, 0)
    resid_slice = lax.dynamic_slice_in_dim(long_resid, first_row, channel_share, 0)
    zero_state = jnp.zeros((channel_share, modes), jnp.float32)
    filtered = by_groups(
        modal_conv, (turned.astype(jnp.float32), rate_slice, resid_slice, zero_state)
    ).astype(jnp.bfloat16)
    long_out = lax.all_to_all(filtered, "ctx", split_axis=1, concat_axis=0, tiled=True).T
    long_out = lax.optimization_barrier(long_out)
    gated = (q_feat * long_out.astype(jnp.float32)).astype(jnp.bfloat16)
    summed_rows = lax.psum_scatter(
        lax.dot_general(
            out_weight, gated, (((0,), (1,)), ((), ())), preferred_element_type=jnp.float32
        ).astype(jnp.bfloat16),
        "tp",
        scatter_dimension=0,
        tiled=True,
    ).astype(jnp.float32)
    return summed_rows.T.astype(jnp.bfloat16)


def solution(mesh):
    return jax.shard_map(
        shards,
        mesh=mesh,
        in_specs=(
            P("ctx", "tp"),
            P("ctx", "tp"),
            P("ctx", "tp"),
            P(None, None, "tp"),
            P("tp", None),
            P("tp", None),
            P("tp", None),
        ),
        out_specs=P("ctx", "tp"),
        check_vma=False,
    )
```

profile of v0, /device:TPU:0, one launch (start us, length us, event | category | flops | bytes accessed | tf_op | source)
XLA Modules:
  0.0 649.2 jit_solution(2100536702451512744)
XLA Ops:
  6.5 0.8 slice.92
  7.4 4.9 collective-permute-start.1
  12.3 0.8 slice.99
  13.0 3.4 collective-permute-start.2
  16.5 1.6 fusion.54
  18.1 1.2 maximum_convert_fusion.1
  19.3 0.1 maximum_convert_fusion.2
  19.4 0.7 fusion.53
  20.1 1.0 copy.48
  21.1 5.1 all-to-all-start
  26.2 0.7 constant_dynamic-slice_fusion.3
  27.0 12.9 %all-to-all-done = bf16[8,256,128]{2,1,0:T(8,128)(2,1)S(1)} async-done(((bf16[8,256,128]{2,1,0:T(8,128)(2,1)}), bf16[8,256,128]{2,1,0:T(8,128)(2,1)S(1)}, u32[]{:S(2)}, u32[]{:S(2)}) %all-to-all-start) | async-done | bytes 524320 | tf_op jit(solution)/shard_map/all_to_all | solution.py:91
  40.0 0.6 copy.49
  40.6 0.2 reshape.184
  40.8 549.3 %while.12 = (s32[]{:T(128)}, bf16[2,128,1024]{2,1,0:T(8,128)(2,1)S(1)}, f32[2,128,1024]{2,1,0:T(8,128)S(1)}, f32[2,128,16]{1,0,2:T(2,128)S(1)}, f32[2,128,16]{1,0,2:T(2,128)S(1)}, /*index=5*/s32[]{:T(128)}) while((s32[]{:T(128)}, bf16[2,128,1024]{2,1,0:T(8,128)(2,1)S(1)}, f32[2,128,1024]{2,1,0:T(8,128)S(1)}, f32[2,128,16]{1,0,2:T(2,128)S(1)}, ...), condition=%wide.region_2.3_spmd, body=%wide.region_0.2_spmd.sunk | while | flops 247787872 | bytes 175966480 | solution.py:33
  40.8 0.1 copy.77
  41.0 0.8 fusion.74
  42.0 0.1 copy.79
  42.2 215.9 %gather_fusion = f32[65536,128]{1,0:T(8,128)} fusion(f32[128,256]{0,1:T(8,128)S(1)} %copy.78, s32[65536]{0:T(1024)S(1)} %broadcast_clamp_fusion.2), kind=kCustom, calls=%fused_computation.clone.1 | custom fusion | bytes 67371008 | tf_op jit(solution)/shard_map/while/body/eval_jaxpr/jit(_take)/gather | solution.py:50
  258.1 33.5 %copy.80 = f32[256,256,128]{1,0,2:T(8,128)} copy(f32[256,256,128]{2,1,0:T(8,128)} %bitcast.82) | data formatting | bytes 67108864 | tf_op jit(solution)/shard_map/while/body/eval_jaxpr/jit(_take)/gather | solution.py:50
  291.6 0.2 reshape.201
  291.9 19.8 %fusion.75 = f32[128,4,256]{2,1,0:T(4,128)S(1)} fusion(f32[128,4,256]{2,1,0:T(4,128)S(1)} %reshape.201, f32[256,256,128]{1,0,2:T(8,128)} %copy.80, pred[256,256]{1,0:T(8,128)(4,1)S(1)} %get-tuple-element.148, pred[256,256]{1,0:T(8,128)(4,1)S(1)} %get-tuple-element.149), kind=kOutput, calls=%fused_computation.1.clone.1 | convolution fusion | flops 218103808 | bytes 34734080 | tf_op jit(solution)/shard_map/while/body/eval_jaxpr/cij,cbj->cbi/dot_general | solution.py:53
  311.8 1.1 fusion.76
  313.0 0.1 multiply_reduce_fusion.2
  313.1 0.1 copy.83
  313.3 0.1 copy.81
  313.4 1.8 fusion.79
  315.2 0.2 broadcast_in_dim.89
  315.7 0.8 fusion.74
  316.6 0.1 copy.79
  316.8 215.9 %gather_fusion = f32[65536,128]{1,0:T(8,128)} fusion(f32[128,256]{0,1:T(8,128)S(1)} %copy.78, s32[65536]{0:T(1024)S(1)} %broadcast_clamp_fusion.2), kind=kCustom, calls=%fused_computation.clone.1 | custom fusion | bytes 67371008 | tf_op jit(solution)/shard_map/while/body/eval_jaxpr/jit(_take)/gather | solution.py:50
  532.7 33.5 %copy.80 = f32[256,256,128]{1,0,2:T(8,128)} copy(f32[256,256,128]{2,1,0:T(8,128)} %bitcast.82) | data formatting | bytes 67108864 | tf_op jit(solution)/shard_map/while/body/eval_jaxpr/jit(_take)/gather | solution.py:50
  566.2 0.2 reshape.201
  566.6 19.8 %fusion.75 = f32[128,4,256]{2,1,0:T(4,128)S(1)} fusion(f32[128,4,256]{2,1,0:T(4,128)S(1)} %reshape.201, f32[256,256,128]{1,0,2:T(8,128)} %copy.80, pred[256,256]{1,0:T(8,128)(4,1)S(1)} %get-tuple-element.148, pred[256,256]{1,0:T(8,128)(4,1)S(1)} %get-tuple-element.149), kind=kOutput, calls=%fused_computation.1.clone.1 | convolution fusion | flops 218103808 | bytes 34734080 | tf_op jit(solution)/shard_map/while/body/eval_jaxpr/cij,cbj->cbi/dot_general | solution.py:53
  586.4 1.1 fusion.76
  587.7 0.1 multiply_reduce_fusion.2
  587.8 0.1 copy.83
  588.1 1.8 fusion.79
  589.9 0.2 broadcast_in_dim.89
  590.2 0.9 copy.52
  591.1 3.8 all-to-all-start.1
  595.0 4.1 collective-permute-start
  599.0 1.2 collective-permute-done
  600.2 0.1 maximum_convert_fusion
  600.3 8.3 %all-to-all-done.1 = bf16[256,8,128]{2,0,1:T(8,128)(2,1)S(1)} async-done(((bf16[256,8,128]{2,0,1:T(8,128)(2,1)}), bf16[256,8,128]{2,0,1:T(8,128)(2,1)S(1)}, u32[]{:S(2)}, u32[]{:S(2)}) %all-to-all-start.1) | async-done | bytes 524320 | tf_op jit(solution)/shard_map/all_to_all | solution.py:99
  608.7 0.2 copy.53
  608.9 9.3 %fusion.38 = bf16[4096,128]{0,1:T(8,128)(2,1)} fusion(bf16[2048,4096]{1,0:T(8,128)(2,1)} %param.15, f32[130,2048]{1,0:T(8,128)S(1)} %maximum_convert_fusion, bf16[128,2048]{1,0:T(8,128)(2,1)S(1)} %bitcast.90, f32[2048]{0:T(1024)S(1)} %bitcast.98, f32[2048]{0:T(1024)S(1)} %bitcast.99, f32[2048]{0:T(1024)S(1)} %bitcast.97), kind=kOutput, calls=%fused_computation.53 | convolution fusion | flops 2150105088 | bytes 21520384 | tf_op jit(solution)/shard_map/dot_general | solution.py:103
  618.2 24.1 %reduce-scatter.2.cloned.1.call-done = bf16[1024,128]{0,1:T(8,128)(2,1)} async-done(((bf16[4096,128]{0,1:T(8,128)(2,1)}), bf16[1024,128]{0,1:T(8,128)(2,1)}) %reduce-scatter.2.cloned.1.call-update) | async-done | bytes 262160 | tf_op jit(solution)/shard_map/reduce_scatter | solution.py:102
  (52 shorter events, 1.6 us)
Async XLA Ops:
  6.5 12.8 %copy-start = (bf16[128,2048]{1,0:T(8,128)(2,1)S(1)}, bf16[128,2048]{1,0:T(8,128)(2,1)}, u32[]{:S(2)}) copy-start(bf16[128,2048]{1,0:T(8,128)(2,1)} %param.11) | copy-start | bytes 1572868
  7.4 10.7 %collective-permute-start.1 = (bf16[2,2048]{1,0:T(2,128)(2,1)S(1)}, bf16[2,2048]{1,0:T(2,128)(2,1)S(1)}, u32[]{:S(2)}, u32[]{:S(2)}) collective-permute-start(bf16[2,2048]{1,0:T(2,128)(2,1)S(1)} %slice.92), channel_id=1, source_target_pairs={{0,4},{4,8},{8,12},{12,16},{16,20},{20,24},{24,28},{1,5},{5,9},{9,... | collective-permute-start | bytes 24584 | tf_op jit(solution)/shard_map/ppermute | solution.py:12
  13.0 6.2 collective-permute-start.2
  21.1 18.8 %all-to-all-start = ((bf16[8,256,128]{2,1,0:T(8,128)(2,1)}), bf16[8,256,128]{2,1,0:T(8,128)(2,1)S(1)}, u32[]{:S(2)}, u32[]{:S(2)}) async-start(bf16[8,256,128]{2,1,0:T(8,128)(2,1)} %bitcast.17), calls=%async_computation | async-start | bytes 1048576 | tf_op jit(solution)/shard_map/all_to_all | solution.py:91
  590.1 4.8 copy-start.1
  591.1 17.8 %copy-start.2 = (f32[1,1,2048]{2,1,0:T(1,128)S(1)}, f32[1,1,2048]{2,1,0:T(1,128)}, u32[]{:S(2)}) copy-start(f32[1,1,2048]{2,1,0:T(1,128)} %get-tuple-element.94) | copy-start | bytes 24580
  591.1 17.8 %copy-start.3 = (f32[1,1,2048]{2,1,0:T(1,128)S(1)}, f32[1,1,2048]{2,1,0:T(1,128)}, u32[]{:S(2)}) copy-start(f32[1,1,2048]{2,1,0:T(1,128)} %get-tuple-element.99) | copy-start | bytes 24580
  591.1 17.8 %copy-start.4 = (f32[1,1,2048]{2,1,0:T(1,128)S(1)}, f32[1,1,2048]{2,1,0:T(1,128)}, u32[]{:S(2)}) copy-start(f32[1,1,2048]{2,1,0:T(1,128)} %get-tuple-element.100) | copy-start | bytes 24580
  591.1 17.6 %all-to-all-start.1 = ((bf16[256,8,128]{2,0,1:T(8,128)(2,1)}), bf16[256,8,128]{2,0,1:T(8,128)(2,1)S(1)}, u32[]{:S(2)}, u32[]{:S(2)}) async-start(bf16[256,8,128]{2,0,1:T(8,128)(2,1)} %copy.52), calls=%async_computation.1 | async-start | bytes 1048576 | tf_op jit(solution)/shard_map/all_to_all | solution.py:99
  594.9 47.4 %reduce-scatter.2.cloned.1.call-start = ((), (), s32[]{:S(2)}) async-start(), calls=%async_computation.3 | async-start | bytes 1310720 | tf_op jit(solution)/shard_map/reduce_scatter | solution.py:102
  595.0 5.2 collective-permute-start
Sparse Core Ops, SparseCore 0:
  618.4 23.9 reduce-scatter.1
where the time goes:
time: 651 us; the launch traced here: 649 us
  local copies, waits for them, and re-layouts  508 us (78%)
  matrix products  54.8 us (8%)
  waiting for transfers between devices  46.5 us (7%)
  starting transfers between devices  21.3 us (3%)
  between operations  13.6 us (2%)
    gather x4, local copies, waits for them, and re-layouts, modal_conv(): toeplitz = jnp.take(kernel, jnp.maximum(offset_table, 0), axis=1)  499 us
    dot_general x2, matrix products, modal_conv(): jnp.einsum('cij,cbj->cbi', toeplitz, blocks_in, precision=better)  39.7 us
    reduce_scatter x1, waiting for transfers between devices, shards(): lax.psum_scatter(lax.dot_general(out_weight, gated, (((0,), (1,)), ((), (...  24.1 us
  transfers between devices with their start and end apart: 6, of which 4 were waited for; matrix products, arithmetic and copies ran while one was open for 1% of the time, Pallas kernels for 0%

commit v1 on v0

v1 whole, which is shorter than its diff:
```python
import functools

import jax
import jax.numpy as jnp
from jax import lax
from jax.experimental import pallas as pl
from jax.experimental.pallas import tpu as pltpu
from jax.sharding import PartitionSpec as P

LANES = 128
VMEM = pltpu.VMEM


def whole():
    return pl.BlockSpec(memory_space=VMEM)


def to_rows(source, target, first, groups):
    count = source.shape[0]
    for group in range(groups):
        piece = source[:, group * LANES : (group + 1) * LANES].astype(jnp.float32)
        target[pl.ds(first * groups + group, count, stride=groups), :] = piece


def spread(stream_ref, halo, target, groups):
    tail = halo.shape[0]
    to_rows(halo, target, 0, groups)
    step = 16

    def body(index, carry):
        start = pl.multiple_of(index * step, step)
        for group in range(groups):
            piece = stream_ref[pl.ds(start, step), group * LANES : (group + 1) * LANES]
            row = (start + tail) * groups + group
            target[pl.ds(row, step, stride=groups), :] = piece.astype(jnp.float32)
        return carry

    lax.fori_loop(0, stream_ref.shape[0] // step, body, 0)


def row_block(index, groups, offset, height):
    start = index * groups + offset
    return pl.ds(pl.multiple_of(start, height), height)


def chunks(groups):
    height = min(8, groups)
    return height, range(0, groups, height)


def state_kernel(tail, groups, halo_ref, k_ref, v_ref, taps_ref, rates_ref, x_ref, state_ref, rate_ref, k_rows, v_rows, tap_rows):
    tokens = k_ref.shape[0]
    modes = rates_ref.shape[0]
    halo = halo_ref[...].astype(jnp.float32)
    spread(k_ref, halo[0:tail], k_rows, groups)
    spread(v_ref, halo[tail : 2 * tail], v_rows, groups)
    to_rows(rates_ref[...], rate_ref, 0, groups)
    taps = tail + 1
    for which in range(2):
        to_rows(taps_ref[1 + which], tap_rows, which * taps, groups)
    height, offsets = chunks(groups)
    for offset in offsets:
        decay = [jnp.exp(-rate_ref[row_block(m, groups, offset, height), :]) for m in range(modes)]
        tap = [tap_rows[row_block(j, groups, offset, height), :] for j in range(2 * taps)]

        def body(position, carry, decay=decay, tap=tap, offset=offset):
            k_old, v_old, state = carry
            k_all = k_old + [k_rows[row_block(position + tail, groups, offset, height), :]]
            v_all = v_old + [v_rows[row_block(position + tail, groups, offset, height), :]]
            k_feat = tap[0] * k_all[tail]
            v_feat = tap[taps] * v_all[tail]
            for j in range(1, taps):
                k_feat = k_feat + tap[j] * k_all[tail - j]
                v_feat = v_feat + tap[taps + j] * v_all[tail - j]
            product = (k_feat * v_feat).astype(jnp.bfloat16).astype(jnp.float32)
            x_ref[row_block(position, groups, offset, height), :] = product
            state = [d * s + product for d, s in zip(decay, state)]
            return k_all[1:], v_all[1:], state

        lead = lambda rows: [rows[row_block(j, groups, offset, height), :] for j in range(tail)]
        zero = [jnp.zeros((height, LANES), jnp.float32)] * modes
        _, _, state = lax.fori_loop(0, tokens, body, (lead(k_rows), lead(v_rows), zero), unroll=4)
        for m in range(modes):
            state_ref[row_block(m, groups, offset, height), :] = state[m]


def local_kernel(tail, groups, halo_ref, q_ref, taps_ref, x_ref, rate_ref, gains_ref, y_ref, qf_ref, gain_ref, q_rows, tap_rows):
    tokens = q_ref.shape[0]
    modes = gains_ref.shape[0]
    taps = tail + 1
    halo = halo_ref[...].astype(jnp.float32)
    spread(q_ref, halo[2 * tail : 3 * tail], q_rows, groups)
    to_rows(gains_ref[...], gain_ref, 0, groups)
    to_rows(taps_ref[0], tap_rows, 0, groups)
    height, offsets = chunks(groups)
    for offset in offsets:
        block = lambda ref, row, offset=offset: ref[row_block(row, groups, offset, height), :]
        tap = [block(tap_rows, j) for j in range(taps)]

        def gate(position, old, tap=tap, offset=offset, block=block):
            rows = old + [block(q_rows, position + tail)]
            feat = tap[0] * rows[tail]
            for j in range(1, taps):
                feat = feat + tap[j] * rows[tail - j]
            qf_ref[row_block(position, groups, offset, height), :] = feat
            return rows[1:]

        lax.fori_loop(0, tokens, gate, [block(q_rows, j) for j in range(tail)], unroll=8)
        decay = [jnp.exp(-block(rate_ref, m)) for m in range(modes)]
        gain = [block(gain_ref, m) for m in range(modes)]

        def body(position, state, decay=decay, gain=gain, offset=offset, block=block):
            product = block(x_ref, position)
            state = [d * s + product for d, s in zip(decay, state)]
            terms = [c * s for c, s in zip(gain, state)]
            while len(terms) > 1:
                terms = [a + b for a, b in zip(terms[::2], terms[1::2])]
            y_ref[row_block(position, groups, offset, height), :] = terms[0]
            return state

        zero = [jnp.zeros((height, LANES), jnp.float32)] * modes
        lax.fori_loop(0, tokens, body, zero, unroll=4)


def carry_kernel(groups, carry_ref, rate_ref, gain_ref, y_ref, qf_ref, gated_ref, rows):
    tokens = gated_ref.shape[0]
    modes = carry_ref.shape[0] // groups
    height, offsets = chunks(groups)
    for offset in offsets:
        block = lambda ref, row, offset=offset: ref[row_block(row, groups, offset, height), :]
        decay = [jnp.exp(-block(rate_ref, m)) for m in range(modes)]
        start = [block(gain_ref, m) * block(carry_ref, m) for m in range(modes)]

        def body(position, state, decay=decay, offset=offset, block=block):
            state = [d * s for d, s in zip(decay, state)]
            terms = list(state)
            while len(terms) > 1:
                terms = [a + b for a, b in zip(terms[::2], terms[1::2])]
            total = block(y_ref, position) + terms[0]
            rounded = total.astype(jnp.bfloat16).astype(jnp.float32)
            rows[row_block(position, groups, offset, height), :] = block(qf_ref, position) * rounded
            return state

        lax.fori_loop(0, tokens, body, start, unroll=4)
    step = 16

    def gather(index, carry):
        begin = pl.multiple_of(index * step, step)
        for group in range(groups):
            piece = rows[pl.ds(begin * groups + group, step, stride=groups), :]
            gated_ref[pl.ds(begin, step), group * LANES : (group + 1) * LANES] = piece.astype(jnp.bfloat16)
        return carry

    lax.fori_loop(0, tokens // step, gather, 0)


def matmul_kernel(which_ref, gated_ref, weight_ref, out_ref):
    del which_ref
    out_ref[...] = jnp.dot(
        gated_ref[...], weight_ref[...], preferred_element_type=jnp.float32
    ).astype(out_ref.dtype)


def project(gated, weight, which, columns, kind):
    tokens, channels = gated.shape
    tile = min(columns, 256)
    steps = columns // tile
    spec = pltpu.PrefetchScalarGridSpec(
        num_scalar_prefetch=1,
        grid=(steps,),
        in_specs=[
            pl.BlockSpec((tokens, channels), lambda i, w: (0, 0)),
            pl.BlockSpec((channels, tile), lambda i, w: (0, w[0] * steps + i)),
        ],
        out_specs=pl.BlockSpec((tokens, tile), lambda i, w: (0, i)),
    )
    return pl.pallas_call(
        matmul_kernel,
        grid_spec=spec,
        out_shape=jax.ShapeDtypeStruct((tokens, columns), kind),
        cost_estimate=pl.CostEstimate(
            flops=2 * tokens * channels * columns,
            bytes_accessed=2 * channels * columns,
            transcendentals=0,
        ),
    )(which.reshape(1), gated, weight)


def swap(value, axis, bits):
    count = lax.axis_size(axis)
    return lax.ppermute(value, axis, [(i, i ^ bits) for i in range(count)])


def radices(count):
    found = []
    while count > 1:
        radix = 2 if not found or count == 2 else 4
        found.append(radix)
        count //= radix
    return found


def carried(state, rate, tokens):
    count = lax.axis_size("ctx")
    index = lax.axis_index("ctx")
    total, before, stride = state, None, 1
    per_device = rate * float(tokens)

    def weight(steps):
        return jnp.exp(-per_device * steps.astype(jnp.float32))

    rounds = radices(count)
    for radix in rounds:
        sent = total.astype(jnp.bfloat16)
        digit = (index // stride) % radix
        others = [(digit ^ j, swap(sent, "ctx", j * stride)) for j in reversed(range(1, radix))]
        inside = index % stride
        new = None
        summed = total * weight(stride * (radix - 1 - digit))
        for place, value in others:
            value = value.astype(jnp.float32)
            steps = jnp.maximum(stride * (digit - 1 - place), 0) + inside
            term = jnp.where(place < digit, weight(steps) * value, 0.0)
            new = term if new is None else new + term
            summed = summed + weight(stride * (radix - 1 - place)) * value
        before = new if before is None else before + new
        total = summed
        stride *= radix
    return jnp.zeros_like(state) if before is None else before


def shards(queries, keys, values, short_taps, long_rates, long_resid, out_weight):
    tokens, channels = queries.shape
    streams, taps, _ = short_taps.shape
    modes = long_rates.shape[1]
    tail = taps - 1
    groups = channels // LANES
    f32 = jnp.float32
    rows = lambda count: jax.ShapeDtypeStruct((count * groups, LANES), f32)
    scratch = lambda count: VMEM((count * groups, LANES), f32)
    ends = jnp.concatenate([item[tokens - tail :] for item in (keys, values, queries)], axis=0)
    count = lax.axis_size("ctx")
    halo = lax.ppermute(ends, "ctx", [(i, i + 1) for i in range(count - 1)])
    rates = long_rates.T
    gains = (long_resid * jnp.sqrt(-jnp.expm1(-2.0 * long_rates))).T
    product, state, rate = pl.pallas_call(
        functools.partial(state_kernel, tail, groups),
        in_specs=[whole()] * 5,
        out_specs=[whole()] * 3,
        out_shape=[rows(tokens), rows(modes), rows(modes)],
        scratch_shapes=[scratch(tokens + tail), scratch(tokens + tail), scratch(2 * taps)],
    )(halo, keys, values, short_taps, rates)
    local, gate, gain = pl.pallas_call(
        functools.partial(local_kernel, tail, groups),
        in_specs=[whole()] * 6,
        out_specs=[whole()] * 3,
        out_shape=[rows(tokens), rows(tokens), rows(modes)],
        scratch_shapes=[scratch(tokens + tail), scratch(taps)],
        cost_estimate=pl.CostEstimate(
            flops=4 * tokens * channels * modes, bytes_accessed=8 * tokens * channels, transcendentals=0
        ),
    )(halo, queries, short_taps, product, rate, gains)
    before = carried(state, rate, tokens)
    gated = pl.pallas_call(
        functools.partial(carry_kernel, groups),
        in_specs=[whole()] * 5,
        out_specs=whole(),
        out_shape=jax.ShapeDtypeStruct((tokens, channels), jnp.bfloat16),
        scratch_shapes=[scratch(tokens)],
    )(before, rate, gain, local, gate)

    parts = lax.axis_size("tp")
    me = lax.axis_index("tp")
    columns = out_weight.shape[1] // parts
    cores = 2 if parts % 2 == 0 else 1
    arrived = []
    own = None
    for chip in reversed(range(0, parts, cores)):
        block = functools.partial(project, gated, out_weight, columns=columns)
        if cores == 2:
            given = swap(block(which=me ^ (chip + 1), kind=jnp.bfloat16), "tp", 1)
            summed = block(which=me ^ chip, kind=f32) + given.astype(f32)
        else:
            summed = block(which=me ^ chip, kind=f32)
        if chip:
            arrived.append(swap(summed.astype(jnp.bfloat16), "tp", chip))
        else:
            own = summed
    for item in arrived:
        own = own + item.astype(f32)
    return own.astype(jnp.bfloat16)


def solution(mesh):
    return jax.shard_map(
        shards,
        mesh=mesh,
        in_specs=(
            P("ctx", "tp"),
            P("ctx", "tp"),
            P("ctx", "tp"),
            P(None, None, "tp"),
            P("tp", None),
            P("tp", None),
            P("tp", None),
        ),
        out_specs=P("ctx", "tp"),
        check_vma=False,
    )
```

time: 651 us -> 67.1 us (0.10)
  local copies, waits for them, and re-layouts: 508 us -> 2.92 us
  matrix products: 54.8 us -> 0 us
  waiting for transfers between devices: 46.5 us -> 5.91 us
  Pallas kernels: 0 us -> 34 us
  between operations: 13.6 us -> 0.06 us
    gather x4 -> x0, local copies, waits for them, and re-layouts: 499 us -> none  [modal_conv(): toeplitz = jnp.take(kernel, jnp.maximum(offset_table, 0), axis=1)]
    dot_general x7 -> x0, matrix products: 54.8 us -> none  [the longest x2 39.7 us: modal_conv(): jnp.einsum('cij,cbj->cbi', toeplitz, blocks_in, precision=better)]
    pallas_call x0 -> x7, Pallas kernels: none -> 34 us  [the longest x4 18.4 us: project(): pl.pallas_call(matmul_kernel, grid_spec=spec, out_shape=jax.ShapeDtypeStr...]
    reduce_scatter x1 -> x0, waiting for transfers between devices: 24.1 us -> none  [shards(): lax.psum_scatter(lax.dot_general(out_weight, gated, (((0,), (1,)), ((), (...]
    all_to_all x2 -> x0, waiting for transfers between devices: 21.3 us -> none  [the longest x1 12.9 us: shards(): lax.all_to_all(product.T, 'ctx', split_axis=0, concat_axis=1, tiled=True)]
    all_to_all x2 -> x0, starting transfers between devices: 8.86 us -> none  [the longest x1 5.08 us: shards(): lax.all_to_all(product.T, 'ctx', split_axis=0, concat_axis=1, tiled=True)]
    ppermute x3 -> x8, starting transfers between devices: 12.4 us -> 15 us  [the longest x7 10.1 us: swap(): return lax.ppermute(value, axis, [(i, i ^ bits) for i in range(count)])]
  transfers between devices with their start and end apart: 6 -> 8, of which waited for: 4 -> 3; matrix products, arithmetic and copies ran while one was open for 1% -> 4% of each run, Pallas kernels for 0% -> 30%
where the time goes in v1:
time: 67.1 us; the launch traced here: 66.2 us
  Pallas kernels  34 us (51%)
  starting transfers between devices  15 us (22%)
  other arithmetic  8.31 us (12%)
  waiting for transfers between devices  5.91 us (9%)
  local copies, waits for them, and re-layouts  2.92 us (4%)
    pallas_call x4, Pallas kernels, project(): pl.pallas_call(matmul_kernel, grid_spec=spec, out_shape=jax.ShapeDtypeStr...  18.4 us
    ppermute x7, starting transfers between devices, swap(): return lax.ppermute(value, axis, [(i, i ^ bits) for i in range(count)])  10.1 us
    pallas_call x1, Pallas kernels, shards(): pl.pallas_call(functools.partial(local_kernel, tail, groups), in_specs=[w...  5.97 us
    pallas_call x1, Pallas kernels, shards(): pl.pallas_call(functools.partial(state_kernel, tail, groups), in_specs=[w...  5.04 us
    ppermute x1, starting transfers between devices, shards(): halo = lax.ppermute(ends, 'ctx', [(i, i + 1) for i in range(count - 1)])  4.9 us
    pallas_call x1, Pallas kernels, shards(): pl.pallas_call(functools.partial(carry_kernel, groups), in_specs=[whole()...  4.53 us
    ppermute x7, waiting for transfers between devices, swap(): return lax.ppermute(value, axis, [(i, i ^ bits) for i in range(count)])  4.33 us
    slice x3, local copies, waits for them, and re-layouts, shards(): item[tokens - tail:]  2.31 us
  transfers between devices with their start and end apart: 8, of which 3 were waited for; matrix products, arithmetic and copies ran while one was open for 4% of the time, Pallas kernels for 30%

profile of v1, /device:TPU:0, one launch (start us, length us, event | category | flops | bytes accessed | tf_op | source)
XLA Modules:
  0.0 66.2 jit_solution(12660154203743956846)
XLA Ops:
  0.0 0.8 %slice.10 = bf16[2,2048]{1,0:T(2,128)(2,1)S(1)} slice(bf16[128,2048]{1,0:T(8,128)(2,1)} %v_ref.1), slice={[126:128], [0:2048]} | slice | bytes 16384 | tf_op jit(solution)/shard_map/slice | solution.py:241
  0.8 0.8 %slice.11 = bf16[2,2048]{1,0:T(2,128)(2,1)S(1)} slice(bf16[128,2048]{1,0:T(8,128)(2,1)} %q_ref.1), slice={[126:128], [0:2048]} | slice | bytes 16384 | tf_op jit(solution)/shard_map/slice | solution.py:241
  1.5 0.8 %slice.9 = bf16[2,2048]{1,0:T(2,128)(2,1)S(1)} slice(bf16[128,2048]{1,0:T(8,128)(2,1)} %k_ref.1), slice={[126:128], [0:2048]} | slice | bytes 16384 | tf_op jit(solution)/shard_map/slice | solution.py:241
  2.4 4.9 %collective-permute-start = (bf16[6,2048]{1,0:T(8,128)(2,1)S(1)}, bf16[6,2048]{1,0:T(8,128)(2,1)S(1)}, u32[]{:S(2)}, u32[]{:S(2)}) collective-permute-start(bf16[6,2048]{1,0:T(8,128)(2,1)S(1)} %pad_maximum_fusion), channel_id=1, source_target_pairs={{0,4},{4,8},{8,12},{12,16},{16,20},{20,24},{24,28},{1,5},{5,9},{9,... | collective-permute-start | bytes 73736 | tf_op jit(solution)/shard_map/ppermute | solution.py:243
  7.3 1.6 %collective-permute-done.halo_ref = bf16[6,2048]{1,0:T(8,128)(2,1)S(1)} collective-permute-done((bf16[6,2048]{1,0:T(8,128)(2,1)S(1)}, bf16[6,2048]{1,0:T(8,128)(2,1)S(1)}, u32[]{:S(2)}, u32[]{:S(2)}) %collective-permute-start) | collective-permute-done | bytes 24608 | tf_op jit(solution)/shard_map/ppermute | solution.py:243
  8.9 0.0 copy-start
  8.9 0.6 copy-done
  9.5 5.0 %shard_map.73 = (f32[2048,128]{1,0:T(8,128)}, f32[256,128]{1,0:T(8,128)}, f32[256,128]{1,0:T(8,128)}) custom-call(bf16[6,2048]{1,0:T(8,128)(2,1)} %copy-done, bf16[128,2048]{1,0:T(8,128)(2,1)} %k_ref.1, bf16[128,2048]{1,0:T(8,128)(2,1)} %v_ref.1, f32[3,3,2048]{2,1,0:T(4,128)} %taps_ref.3, f32[16,2048]{1,0:T(8,128)} %bitcast.7), custom_call_target="tpu_custom_call" | custom-call | tf_op jit(solution)/shard_map/pallas_call | solution.py:246
  14.5 0.9 %convert_element_type.52 = bf16[256,128]{1,0:T(8,128)(2,1)S(1)} convert(f32[256,128]{1,0:T(8,128)} %get-tuple-element.12) | non-fusion elementwise | flops 32768 | bytes 196608 | tf_op jit(solution)/shard_map/convert_element_type | solution.py:214
  15.4 2.3 %collective-permute-start.1 = (bf16[256,128]{1,0:T(8,128)(2,1)S(1)}, bf16[256,128]{1,0:T(8,128)(2,1)S(1)}, u32[]{:S(2)}, u32[]{:S(2)}) collective-permute-start(bf16[256,128]{1,0:T(8,128)(2,1)S(1)} %convert_element_type.52), channel_id=1, source_target_pairs={{0,4},{4,0},{8,12},{12,8},{16,20},{20,16},{24,28},{28,24},{1,5},{5... | collective-permute-start | bytes 196616 | tf_op jit(solution)/shard_map/ppermute | solution.py:191
  17.7 2.2 %collective-permute-done.1 = bf16[256,128]{1,0:T(8,128)(2,1)S(1)} collective-permute-done((bf16[256,128]{1,0:T(8,128)(2,1)S(1)}, bf16[256,128]{1,0:T(8,128)(2,1)S(1)}, u32[]{:S(2)}, u32[]{:S(2)}) %collective-permute-start.1) | collective-permute-done | bytes 65568 | tf_op jit(solution)/shard_map/ppermute | solution.py:191
  20.0 1.0 %fusion.3 = bf16[256,128]{1,0:T(8,128)(2,1)S(1)} fusion(bf16[256,128]{1,0:T(8,128)(2,1)S(1)} %collective-permute-done.1, f32[256,128]{1,0:T(8,128)} %get-tuple-element.12, f32[256,128]{1,0:T(8,128)} %get-tuple-element.11.rate_ref, f32[]{:T(128)S(6)} %convert_element_type.56, f32[]{:T(128)S(6)} %convert_element_type.55), kind=kLoop, calls=%fused_computation.7 | loop fusion | flops 294912 | bytes 393224 | tf_op jit(solution)/shard_map/convert_element_type | solution.py:214
  21.0 5.1 %collective-permute-start.2 = (bf16[256,128]{1,0:T(8,128)(2,1)S(1)}, bf16[256,128]{1,0:T(8,128)(2,1)S(1)}, u32[]{:S(2)}, u32[]{:S(2)}) collective-permute-start(bf16[256,128]{1,0:T(8,128)(2,1)S(1)} %fusion.3), channel_id=1, source_target_pairs={{0,24},{4,28},{8,16},{12,20},{16,8},{20,12},{24,0},{28,4},{1,25},{... | collective-permute-start | bytes 196616 | tf_op jit(solution)/shard_map/ppermute | solution.py:191
  26.1 0.0 collective-permute-start.3
  26.1 0.6 collective-permute-start.4
  26.7 1.7 %multiply_bitcast_fusion.gains_ref = f32[16,2048]{1,0:T(8,128)} fusion(f32[2048,16]{0,1:T(8,128)} %param.12, f32[2048,16]{0,1:T(8,128)} %param.11), kind=kLoop, calls=%fused_computation.8 | loop fusion | flops 98304 | bytes 393216 | tf_op jit(solution)/shard_map/transpose | solution.py:245
  28.4 6.0 %shard_map.74 = (f32[2048,128]{1,0:T(8,128)}, f32[2048,128]{1,0:T(8,128)}, f32[256,128]{1,0:T(8,128)}) custom-call(bf16[6,2048]{1,0:T(8,128)(2,1)} %copy-done, bf16[128,2048]{1,0:T(8,128)(2,1)} %q_ref.1, f32[3,3,2048]{2,1,0:T(4,128)} %taps_ref.3, f32[2048,128]{1,0:T(8,128)} %get-tuple-element.13.x_ref, f32[256,128]{1,0:T(8,128)} %get-tuple-element.11.rate_ref, ...), custom_call_target="tpu_custom_call" | custom-call | flops 16777216 | bytes 2097152 | tf_op jit(solution)/shard_map/pallas_call | solution.py:253
  34.4 0.0 collective-permute-done.2
  34.4 0.0 collective-permute-done.3
  34.4 0.0 collective-permute-done.4
  34.4 1.7 %fusion.1.carry_ref = f32[256,128]{1,0:T(8,128)} fusion(bf16[256,128]{1,0:T(8,128)(2,1)S(1)} %collective-permute-done.1, bf16[256,128]{1,0:T(8,128)(2,1)S(1)} %collective-permute-done.4, bf16[256,128]{1,0:T(8,128)(2,1)S(1)} %collective-permute-done.3, bf16[256,128]{1,0:T(8,128)(2,1)S(1)} %collective-permute-done.2, f32[256,128]{1,0:T(8,128)} %get-tuple-element.11.rate_ref, ...), kind=kLoop, calls=%fused_computation.5 | loop fusion | flops 688128 | bytes 524308 | tf_op jit(solution)/shard_map/add | solution.py:226
  36.1 4.5 %shard_map.75.gated_ref = bf16[128,2048]{1,0:T(8,128)(2,1)} custom-call(f32[256,128]{1,0:T(8,128)} %fusion.1.carry_ref, f32[256,128]{1,0:T(8,128)} %get-tuple-element.11.rate_ref, f32[256,128]{1,0:T(8,128)} %get-tuple-element.14.gain_ref, f32[2048,128]{1,0:T(8,128)} %get-tuple-element.15.y_ref, f32[2048,128]{1,0:T(8,128)} %get-tuple-element.16.qf_ref), custom_call_target="tpu_custom_call" | custom-call | tf_op jit(solution)/shard_map/pallas_call | solution.py:264
  40.6 4.6 %shard_map.79 = bf16[128,1024]{1,0:T(8,128)(2,1)} custom-call(s32[1]{0:T(128)} %bitcast.5.which_ref, bf16[128,2048]{1,0:T(8,128)(2,1)} %shard_map.75.gated_ref, bf16[2048,4096]{1,0:T(8,128)(2,1)} %weight_ref.7), custom_call_target="tpu_custom_call" | custom-call | flops 536870912 | bytes 4194304 | tf_op jit(solution)/shard_map/pallas_call | solution.py:177
  45.2 0.0 collective-permute-start.6
  45.2 4.6 %shard_map.77 = bf16[128,1024]{1,0:T(8,128)(2,1)} custom-call(s32[1]{0:T(128)} %bitcast.3.which_ref, bf16[128,2048]{1,0:T(8,128)(2,1)} %shard_map.75.gated_ref, bf16[2048,4096]{1,0:T(8,128)(2,1)} %weight_ref.7), custom_call_target="tpu_custom_call" | custom-call | flops 536870912 | bytes 4194304 | tf_op jit(solution)/shard_map/pallas_call | solution.py:177
  49.8 0.5 collective-permute-start.5
  50.3 4.7 %shard_map.78 = f32[128,1024]{1,0:T(8,128)} custom-call(s32[1]{0:T(128)} %bitcast.4.which_ref, bf16[128,2048]{1,0:T(8,128)(2,1)} %shard_map.75.gated_ref, bf16[2048,4096]{1,0:T(8,128)(2,1)} %weight_ref.7), custom_call_target="tpu_custom_call" | custom-call | flops 536870912 | bytes 4194304 | tf_op jit(solution)/shard_map/pallas_call | solution.py:177
  54.9 0.0 collective-permute-done.6
  54.9 1.1 %add_convert_fusion.1 = bf16[128,1024]{1,0:T(8,128)(2,1)S(1)} fusion(f32[128,1024]{1,0:T(8,128)} %shard_map.78, bf16[128,1024]{1,0:T(8,128)(2,1)S(1)} %collective-permute-done.6), kind=kLoop, calls=%fused_computation.1 | loop fusion | flops 393216 | bytes 1048576 | tf_op jit(solution)/shard_map/convert_element_type | solution.py:286
  56.0 1.6 %collective-permute-start.7 = (bf16[128,1024]{1,0:T(8,128)(2,1)S(1)}, bf16[128,1024]{1,0:T(8,128)(2,1)S(1)}, u32[]{:S(2)}, u32[]{:S(2)}) collective-permute-start(bf16[128,1024]{1,0:T(8,128)(2,1)S(1)} %add_convert_fusion.1), channel_id=1, source_target_pairs={{0,2},{1,3},{2,0},{3,1},{4,6},{5,7},{6,4},{7,5},{8,10},{9,11},{10,... | collective-permute-start | bytes 786440 | tf_op jit(solution)/shard_map/ppermute | solution.py:191
  57.6 4.7 %shard_map.76 = f32[128,1024]{1,0:T(8,128)} custom-call(s32[1]{0:T(128)} %bitcast.which_ref, bf16[128,2048]{1,0:T(8,128)(2,1)} %shard_map.75.gated_ref, bf16[2048,4096]{1,0:T(8,128)(2,1)} %weight_ref.7), custom_call_target="tpu_custom_call" | custom-call | flops 536870912 | bytes 4194304 | tf_op jit(solution)/shard_map/pallas_call | solution.py:177
  62.2 0.0 collective-permute-done.5
  62.2 2.1 %collective-permute-done.7 = bf16[128,1024]{1,0:T(8,128)(2,1)S(1)} collective-permute-done((bf16[128,1024]{1,0:T(8,128)(2,1)S(1)}, bf16[128,1024]{1,0:T(8,128)(2,1)S(1)}, u32[]{:S(2)}, u32[]{:S(2)}) %collective-permute-start.7) | collective-permute-done | bytes 262176 | tf_op jit(solution)/shard_map/ppermute | solution.py:191
  64.3 1.8 %add_convert_fusion = bf16[128,1024]{1,0:T(8,128)(2,1)} fusion(bf16[128,1024]{1,0:T(8,128)(2,1)S(1)} %collective-permute-done.7, f32[128,1024]{1,0:T(8,128)} %shard_map.76, bf16[128,1024]{1,0:T(8,128)(2,1)S(1)} %collective-permute-done.5), kind=kLoop, calls=%fused_computation | loop fusion | flops 655360 | bytes 1310720 | tf_op jit(solution)/shard_map/convert_element_type | solution.py:291
  (1 shorter events, 0.0 us)
Async XLA Ops:
  2.4 6.5 %collective-permute-start = (bf16[6,2048]{1,0:T(8,128)(2,1)S(1)}, bf16[6,2048]{1,0:T(8,128)(2,1)S(1)}, u32[]{:S(2)}, u32[]{:S(2)}) collective-permute-start(bf16[6,2048]{1,0:T(8,128)(2,1)S(1)} %pad_maximum_fusion), channel_id=1, source_target_pairs={{0,4},{4,8},{8,12},{12,16},{16,20},{20,24},{24,28},{1,5},{5,9},{9,... | collective-permute-start | bytes 73736 | tf_op jit(solution)/shard_map/ppermute | solution.py:243
  8.9 0.6 copy-start
  15.4 4.6 %collective-permute-start.1 = (bf16[256,128]{1,0:T(8,128)(2,1)S(1)}, bf16[256,128]{1,0:T(8,128)(2,1)S(1)}, u32[]{:S(2)}, u32[]{:S(2)}) collective-permute-start(bf16[256,128]{1,0:T(8,128)(2,1)S(1)} %convert_element_type.52), channel_id=1, source_target_pairs={{0,4},{4,0},{8,12},{12,8},{16,20},{20,16},{24,28},{28,24},{1,5},{5... | collective-permute-start | bytes 196616 | tf_op jit(solution)/shard_map/ppermute | solution.py:191
  21.0 13.4 %collective-permute-start.2 = (bf16[256,128]{1,0:T(8,128)(2,1)S(1)}, bf16[256,128]{1,0:T(8,128)(2,1)S(1)}, u32[]{:S(2)}, u32[]{:S(2)}) collective-permute-start(bf16[256,128]{1,0:T(8,128)(2,1)S(1)} %fusion.3), channel_id=1, source_target_pairs={{0,24},{4,28},{8,16},{12,20},{16,8},{20,12},{24,0},{28,4},{1,25},{... | collective-permute-start | bytes 196616 | tf_op jit(solution)/shard_map/ppermute | solution.py:191
  26.1 8.3 %collective-permute-start.3 = (bf16[256,128]{1,0:T(8,128)(2,1)S(1)}, bf16[256,128]{1,0:T(8,128)(2,1)S(1)}, u32[]{:S(2)}, u32[]{:S(2)}) collective-permute-start(bf16[256,128]{1,0:T(8,128)(2,1)S(1)} %fusion.3), channel_id=1, source_target_pairs={{0,16},{4,20},{8,24},{12,28},{16,0},{20,4},{24,8},{28,12},{1,17},{... | collective-permute-start | bytes 196616 | tf_op jit(solution)/shard_map/ppermute | solution.py:191
  26.1 8.3 %collective-permute-start.4 = (bf16[256,128]{1,0:T(8,128)(2,1)S(1)}, bf16[256,128]{1,0:T(8,128)(2,1)S(1)}, u32[]{:S(2)}, u32[]{:S(2)}) collective-permute-start(bf16[256,128]{1,0:T(8,128)(2,1)S(1)} %fusion.3), channel_id=1, source_target_pairs={{0,8},{4,12},{8,0},{12,4},{16,24},{20,28},{24,16},{28,20},{1,9},{5... | collective-permute-start | bytes 196616 | tf_op jit(solution)/shard_map/ppermute | solution.py:191
  45.2 9.7 %collective-permute-start.6 = (bf16[128,1024]{1,0:T(8,128)(2,1)}, bf16[128,1024]{1,0:T(8,128)(2,1)S(1)}, u32[]{:S(2)}, u32[]{:S(2)}) collective-permute-start(bf16[128,1024]{1,0:T(8,128)(2,1)} %shard_map.79), channel_id=1, source_target_pairs={{0,1},{1,0},{2,3},{3,2},{4,5},{5,4},{6,7},{7,6},{8,9},{9,8},{10,11... | collective-permute-start | bytes 786440 | tf_op jit(solution)/shard_map/ppermute | solution.py:191
  49.8 12.5 %collective-permute-start.5 = (bf16[128,1024]{1,0:T(8,128)(2,1)}, bf16[128,1024]{1,0:T(8,128)(2,1)S(1)}, u32[]{:S(2)}, u32[]{:S(2)}) collective-permute-start(bf16[128,1024]{1,0:T(8,128)(2,1)} %shard_map.77), channel_id=1, source_target_pairs={{0,1},{1,0},{2,3},{3,2},{4,5},{5,4},{6,7},{7,6},{8,9},{9,8},{10,11... | collective-permute-start | bytes 786440 | tf_op jit(solution)/shard_map/ppermute | solution.py:191
  56.0 8.3 %collective-permute-start.7 = (bf16[128,1024]{1,0:T(8,128)(2,1)S(1)}, bf16[128,1024]{1,0:T(8,128)(2,1)S(1)}, u32[]{:S(2)}, u32[]{:S(2)}) collective-permute-start(bf16[128,1024]{1,0:T(8,128)(2,1)S(1)} %add_convert_fusion.1), channel_id=1, source_target_pairs={{0,2},{1,3},{2,0},{3,1},{4,6},{5,7},{6,4},{7,5},{8,10},{9,11},{10,... | collective-permute-start | bytes 786440 | tf_op jit(solution)/shard_map/ppermute | solution.py:191

commit v2 on v0

v2 whole, which is shorter than its diff:
```python
import functools

import jax
import jax.numpy as jnp
from jax import lax
from jax.experimental import pallas as pl
from jax.experimental.pallas import tpu as pltpu
from jax.sharding import PartitionSpec as P

LANES = 128
SUBLANES = 8
VMEM = pltpu.VMEM
SMALL = pltpu.CompilerParams(vmem_limit_bytes=8 * 2**20)
F32, BF16 = jnp.float32, jnp.bfloat16


def here():
    return pl.BlockSpec(memory_space=VMEM)


def far():
    return pl.BlockSpec(memory_space=pltpu.HBM)


def factor(count, most):
    return max(size for size in range(1, most + 1) if count % size == 0)


def at(row, height):
    return pl.ds(pl.multiple_of(row * height, height), height)


def to_rows(source, target, first, part, height):
    count = source.shape[0]
    for group in range(height):
        lane = (part * height + group) * LANES
        target[pl.ds(first * height + group, count, stride=height), :] = source[:, lane : lane + LANES].astype(F32)


def spread(stream_ref, target, first, part, height):
    step = 16

    def body(index, carry):
        start = pl.multiple_of(index * step, step)
        to_rows(stream_ref.at[pl.ds(start, step)], target, first + start, part, height)
        return carry

    lax.fori_loop(0, stream_ref.shape[0] // step, body, 0)


def summed(terms):
    terms = list(terms)
    while len(terms) > 1:
        pairs = [a + b for a, b in zip(terms[::2], terms[1::2])]
        terms = pairs + terms[2 * len(pairs) :]
    return terms[0]


def convolved(taps, rows):
    return summed(tap * row for tap, row in zip(taps, reversed(rows)))


def rounded(value):
    return value.astype(BF16).astype(F32)


def fetch_kernel(tail, *refs):
    count = (len(refs) - 2) // 2
    sources, (ends_ref, *targets), sems = refs[:count], refs[count:-1], refs[-1]
    copies = [pltpu.make_async_copy(s, t, sems.at[i]) for i, (s, t) in enumerate(zip(sources, targets))]
    for copy in copies:
        copy.start()
    for copy in copies:
        copy.wait()
    tokens = targets[0].shape[0]
    last = [ref[tokens - 16 :, :].astype(F32)[16 - tail :] for ref in targets[:3]]
    ends_ref[...] = jnp.concatenate(last, axis=0).astype(BF16)


def state_kernel(tail, height, k_ref, v_ref, taps_ref, rates_ref, weight_ref, x_ref, state_ref, rate_ref, tap_ref, piece_ref, k_rows, v_rows, sem):
    rows = piece_ref.shape[0]
    copy = pltpu.make_async_copy(weight_ref.at[pl.ds(0, rows)], piece_ref, sem)
    copy.start()
    tokens, channels = k_ref.shape
    modes = rates_ref.shape[0]
    taps = tail + 1
    for part in range(channels // (height * LANES)):
        spread(k_ref, k_rows, 0, part, height)
        spread(v_ref, v_rows, 0, part, height)
        to_rows(rates_ref[...], rate_ref, part * modes, part, height)
        for which in range(2):
            to_rows(taps_ref[1 + which], tap_ref, (2 * part + which) * taps, part, height)
        decay = [jnp.exp(-rate_ref[at(part * modes + m, height), :]) for m in range(modes)]
        tap = [tap_ref[at(2 * part * taps + j, height), :] for j in range(2 * taps)]

        def body(position, carry, decay=decay, tap=tap, part=part):
            k_old, v_old, state = carry
            k_all = k_old + [k_rows[at(position, height), :]]
            v_all = v_old + [v_rows[at(position, height), :]]
            product = rounded(convolved(tap[:taps], k_all) * convolved(tap[taps:], v_all))
            x_ref[at(part * tokens + position, height), :] = product
            return k_all[1:], v_all[1:], [d * s + product for d, s in zip(decay, state)]

        lead = lambda rows: [rows[at(j, height), :] for j in range(tail)]
        zero = [jnp.zeros((height, LANES), F32)] * modes
        first = (lead(k_rows), lead(v_rows), zero)
        state = lax.fori_loop(tail, tokens, body, first, unroll=factor(tokens - tail, 8))[2]
        for m in range(modes):
            state_ref[at(part * modes + m, height), :] = state[m]
    copy.wait()


def first_kernel(tail, height, halo_ref, k_ref, v_ref, tap_ref, rate_ref, part_state_ref, start_ref, state_ref, sent_ref, k_rows, v_rows):
    tokens, channels = k_ref.shape
    taps = tail + 1
    parts = channels // (height * LANES)
    modes = rate_ref.shape[0] // (height * parts)
    halo = halo_ref[...].astype(F32)
    for part in range(parts):
        for which, (ref, rows) in enumerate(((k_ref, k_rows), (v_ref, v_rows))):
            to_rows(halo[which * tail : (which + 1) * tail], rows, 0, part, height)
            to_rows(ref[0:16].astype(F32)[:tail], rows, tail, part, height)
        tap = [tap_ref[at(2 * part * taps + j, height), :] for j in range(2 * taps)]
        products = []
        for position in range(tail):
            near = lambda rows: [rows[at(position + j, height), :] for j in range(taps)]
            product = rounded(convolved(tap[:taps], near(k_rows)) * convolved(tap[taps:], near(v_rows)))
            start_ref[at(part * tail + position, height), :] = product
            products.append(product)
        for m in range(modes):
            here_ = at(part * modes + m, height)
            rate = rate_ref[here_, :]
            late = [jnp.exp(-rate * float(tokens - 1 - j)) * product for j, product in enumerate(products)]
            state_ref[here_, :] = part_state_ref[here_, :] + summed(late)
    sent_ref[...] = state_ref[...].astype(BF16)


def gain_of(rate, resid):
    twice = 2.0 * rate
    series = jnp.ones_like(twice)
    for order in range(9, 1, -1):
        series = 1.0 - twice * (1.0 / order) * series
    return resid * jnp.sqrt(jnp.where(twice < 0.25, twice * series, 1.0 - jnp.exp(-twice)))


def local_kernel(part, tail, height, halo_ref, q_ref, taps_ref, resid_ref, rate_ref, x_ref, start_ref, weight_ref, y_ref, qf_ref, gain_ref, piece_ref, q_rows, tap_rows, sem):
    tokens, channels = q_ref.shape
    modes = resid_ref.shape[0]
    taps = tail + 1
    parts = channels // (height * LANES)
    rows = piece_ref.shape[0]
    begin = weight_ref.shape[0] - (parts - part) * rows
    copy = pltpu.make_async_copy(weight_ref.at[pl.ds(begin, rows)], piece_ref, sem)
    copy.start()
    to_rows(halo_ref[...].astype(F32)[2 * tail : 3 * tail], q_rows, 0, part, height)
    spread(q_ref, q_rows, tail, part, height)
    to_rows(resid_ref[...], gain_ref, 0, part, height)
    to_rows(taps_ref[0], tap_rows, 0, part, height)
    tap = [tap_rows[at(j, height), :] for j in range(taps)]

    def gate(position, old):
        rows = old + [q_rows[at(position + tail, height), :]]
        qf_ref[at(position, height), :] = convolved(tap, rows)
        return rows[1:]

    lax.fori_loop(0, tokens, gate, [q_rows[at(j, height), :] for j in range(tail)], unroll=8)
    rates = [rate_ref[at(part * modes + m, height), :] for m in range(modes)]
    gain = [gain_of(rate, gain_ref[at(m, height), :]) for m, rate in enumerate(rates)]
    for m in range(modes):
        gain_ref[at(m, height), :] = gain[m]
    decay = [jnp.exp(-rate) for rate in rates]

    def step(position, state, product):
        state = [d * s + product for d, s in zip(decay, state)]
        y_ref[at(position, height), :] = summed(c * s for c, s in zip(gain, state))
        return state

    state = [jnp.zeros((height, LANES), F32)] * modes
    for position in range(tail):
        state = step(position, state, start_ref[at(part * tail + position, height), :])
    body = lambda position, state: step(position, state, x_ref[at(part * tokens + position, height), :])
    lax.fori_loop(tail, tokens, body, state, unroll=factor(tokens - tail, 8))
    copy.wait()


def weight_of(tokens, rate_ref, devices):
    return jnp.exp(-rate_ref[...] * (tokens * devices).astype(F32))


def before_of(tokens, stride, radix, rate_ref, before_ref, others):
    index = lax.axis_index("ctx")
    digit, inside = (index // stride) % radix, index % stride
    terms = [before_ref[...]]
    for j, ref in enumerate(others, 1):
        place = digit ^ j
        steps = jnp.maximum(stride * (digit - 1 - place), 0) + inside
        scale = jnp.where(place < digit, 1.0, 0.0)
        terms.append(weight_of(tokens, rate_ref, steps) * (scale * ref[...].astype(F32)))
    return summed(terms)


def join_kernel(tokens, stride, radix, rate_ref, total_ref, before_ref, *refs):
    others, (joined_ref, sent_ref, next_ref) = refs[:-3], refs[-3:]
    next_ref[...] = before_of(tokens, stride, radix, rate_ref, before_ref, others)
    digit = (lax.axis_index("ctx") // stride) % radix
    terms = [weight_of(tokens, rate_ref, stride * (radix - 1 - digit)) * total_ref[...]]
    for j, ref in enumerate(others, 1):
        terms.append(weight_of(tokens, rate_ref, stride * (radix - 1 - (digit ^ j))) * ref[...].astype(F32))
    joined_ref[...] = summed(terms)
    sent_ref[...] = joined_ref[...].astype(BF16)


def carry_kernel(height, stride, radix, rate_ref, before_ref, *refs):
    gated_ref, carry_ref, rows = refs[-3:]
    tokens = gated_ref.shape[0]
    others, refs = refs[: radix - 1], refs[radix - 1 : -3]
    carry_ref[...] = before_of(tokens, stride, radix, rate_ref, before_ref, others)
    parts = len(refs) // 3
    modes = rate_ref.shape[0] // (height * parts)
    for part in range(parts):
        y_ref, qf_ref, gain_ref = refs[3 * part : 3 * part + 3]
        decay = [jnp.exp(-rate_ref[at(part * modes + m, height), :]) for m in range(modes)]
        start = [gain_ref[at(m, height), :] * carry_ref[at(part * modes + m, height), :] for m in range(modes)]

        def body(position, state, decay=decay, y_ref=y_ref, qf_ref=qf_ref):
            here_ = at(position, height)
            state = [d * s for d, s in zip(decay, state)]
            rows[here_, :] = qf_ref[here_, :] * rounded(y_ref[here_, :] + summed(state))
            return state

        lax.fori_loop(0, tokens, body, start, unroll=8)
        step = 16

        def gather(index, carry, part=part):
            begin = pl.multiple_of(index * step, step)
            for group in range(height):
                lane = (part * height + group) * LANES
                piece = rows[pl.ds(begin * height + group, step, stride=height), :]
                gated_ref[pl.ds(begin, step), lane : lane + LANES] = piece.astype(BF16)
            return carry

        lax.fori_loop(0, tokens // step, gather, 0)


def matmul_kernel(bits, gated_ref, *refs):
    out_ref = refs[-1]
    columns = out_ref.shape[1]
    block = pl.ds(pl.multiple_of((lax.axis_index("tp") ^ bits) * columns, LANES), columns)
    first, total = 0, None
    for piece_ref in refs[:-1]:
        rows = piece_ref.shape[0]
        term = jnp.dot(gated_ref[:, first : first + rows], piece_ref[:, block], preferred_element_type=F32)
        total = term if total is None else total + term
        first += rows
    out_ref[...] = total.astype(out_ref.dtype)


def project(gated, pieces, bits, columns, kind):
    tokens, channels = gated.shape
    return pl.pallas_call(
        functools.partial(matmul_kernel, bits),
        in_specs=[here()] * (1 + len(pieces)),
        out_specs=here(),
        out_shape=jax.ShapeDtypeStruct((tokens, columns), kind),
        compiler_params=SMALL,
        cost_estimate=pl.CostEstimate(
            flops=2 * tokens * channels * columns,
            bytes_accessed=2 * channels * columns,
            transcendentals=0,
        ),
    )(gated, *pieces)


def swap(value, axis, bits):
    count = lax.axis_size(axis)
    return lax.ppermute(value, axis, [(i, i ^ bits) for i in range(count)])


def radices(count):
    found = []
    while count > 1:
        found.append(2 if not found or count == 2 else 4)
        count //= found[-1]
    return found


def exchange(sent, stride, radix):
    far_first = {j: swap(sent, "ctx", j * stride) for j in reversed(range(1, radix))}
    return [far_first[j] for j in range(1, radix)]


def shards(queries, keys, values, short_taps, long_rates, long_resid, out_weight):
    tokens, channels = queries.shape
    taps = short_taps.shape[1]
    modes = long_rates.shape[1]
    tail = taps - 1
    height = min(SUBLANES, channels // LANES)
    parts = channels // (height * LANES)
    shape = jax.ShapeDtypeStruct
    rows = lambda count, kind=F32: shape((count * height, LANES), kind)
    scratch = lambda count: VMEM((count * height, LANES), F32)

    out_weight = pltpu.with_memory_space_constraint(out_weight, pltpu.HBM)
    arguments = (keys, values, queries, short_taps, long_rates.T, long_resid.T)
    ends, keys, values, queries, short_taps, rates, resid = pl.pallas_call(
        functools.partial(fetch_kernel, tail),
        in_specs=[far()] * len(arguments),
        out_specs=[here()] * (1 + len(arguments)),
        out_shape=[shape((3 * tail, channels), BF16)] + [shape(a.shape, a.dtype) for a in arguments],
        scratch_shapes=[pltpu.SemaphoreType.DMA((len(arguments),))],
        compiler_params=SMALL,
    )(*[pltpu.with_memory_space_constraint(a, pltpu.HBM) for a in arguments])
    count = lax.axis_size("ctx")
    halo = lax.ppermute(ends, "ctx", [(i, i + 1) for i in range(count - 1)])

    product, part_state, rate, tap, piece = pl.pallas_call(
        functools.partial(state_kernel, tail, height),
        in_specs=[here()] * 4 + [far()],
        out_specs=[here()] * 5,
        out_shape=[
            rows(parts * tokens),
            rows(parts * modes),
            rows(parts * modes),
            rows(parts * 2 * taps),
            shape((channels // 2, out_weight.shape[1]), BF16),
        ],
        scratch_shapes=[scratch(tokens), scratch(tokens), pltpu.SemaphoreType.DMA],
        compiler_params=SMALL,
        cost_estimate=pl.CostEstimate(flops=2 * tokens * channels * modes, bytes_accessed=channels * out_weight.shape[1], transcendentals=0),
    )(keys, values, short_taps, rates, out_weight)
    pieces = [piece]

    start, total, sent = pl.pallas_call(
        functools.partial(first_kernel, tail, height),
        in_specs=[here()] * 6,
        out_specs=[here()] * 3,
        out_shape=[rows(parts * tail), rows(parts * modes), rows(parts * modes, BF16)],
        scratch_shapes=[scratch(tail + taps), scratch(tail + taps)],
        compiler_params=SMALL,
    )(halo, keys, values, tap, rate, part_state)

    local = []
    for part in range(parts):
        *found, piece = pl.pallas_call(
            functools.partial(local_kernel, part, tail, height),
            in_specs=[here()] * 7 + [far()],
            out_specs=[here()] * 4,
            out_shape=[
                rows(tokens),
                rows(tokens),
                rows(modes),
                shape((channels // (2 * parts), out_weight.shape[1]), BF16),
            ],
            scratch_shapes=[scratch(tokens + tail), scratch(taps), pltpu.SemaphoreType.DMA],
            compiler_params=SMALL,
            cost_estimate=pl.CostEstimate(
                flops=4 * tokens * channels * modes // parts, bytes_accessed=channels * out_weight.shape[1] // parts, transcendentals=0
            ),
        )(halo, queries, short_taps, resid, rate, product, start, out_weight)
        local += found
        pieces.append(piece)

    before = jnp.zeros((parts * modes * height, LANES), F32)
    stride = 1
    steps = radices(count) or [1]
    for radix in steps[:-1]:
        others = exchange(sent, stride, radix)
        total, sent, before = pl.pallas_call(
            functools.partial(join_kernel, tokens, stride, radix),
            in_specs=[here()] * (3 + len(others)),
            out_specs=[here()] * 3,
            out_shape=[rows(parts * modes), rows(parts * modes, BF16), rows(parts * modes)],
            compiler_params=SMALL,
        )(rate, total, before, *others)
        stride *= radix
    others = exchange(sent, stride, steps[-1])
    gated = pl.pallas_call(
        functools.partial(carry_kernel, height, stride, steps[-1]),
        in_specs=[here()] * (2 + len(others) + len(local)),
        out_specs=here(),
        out_shape=shape((tokens, channels), BF16),
        scratch_shapes=[scratch(parts * modes), scratch(tokens)],
        compiler_params=SMALL,
    )(rate, before, *others, *local)

    ranks = lax.axis_size("tp")
    columns = out_weight.shape[1] // ranks
    cores = 2 if ranks % 2 == 0 else 1
    arrived = []
    own = None
    for chip in reversed(range(0, ranks, cores)):
        block = functools.partial(project, gated, pieces, columns=columns)
        if cores == 2:
            given = swap(block(bits=chip + 1, kind=BF16), "tp", 1)
            total = block(bits=chip, kind=F32) + given.astype(F32)
        else:
            total = block(bits=chip, kind=F32)
        if chip:
            arrived.append(swap(total.astype(BF16), "tp", chip))
        else:
            own = total
    for item in arrived:
        own = own + item.astype(F32)
    return own.astype(BF16)


def solution(mesh):
    return jax.shard_map(
        shards,
        mesh=mesh,
        in_specs=(
            P("ctx", "tp"),
            P("ctx", "tp"),
            P("ctx", "tp"),
            P(None, None, "tp"),
            P("tp", None),
            P("tp", None),
            P("tp", None),
        ),
        out_specs=P("ctx", "tp"),
        check_vma=False,
    )
```

time: 651 us -> 39.4 us (0.06)
  local copies, waits for them, and re-layouts: 508 us -> 0.01 us
  matrix products: 54.8 us -> 0 us
  waiting for transfers between devices: 46.5 us -> 10.2 us
  Pallas kernels: 0 us -> 14.9 us
  between operations: 13.6 us -> 0.15 us
  starting transfers between devices: 21.3 us -> 13.1 us
    gather x4 -> x0, local copies, waits for them, and re-layouts: 499 us -> none  [modal_conv(): toeplitz = jnp.take(kernel, jnp.maximum(offset_table, 0), axis=1)]
    dot_general x7 -> x0, matrix products: 54.8 us -> none  [the longest x2 39.7 us: modal_conv(): jnp.einsum('cij,cbj->cbi', toeplitz, blocks_in, precision=better)]
    reduce_scatter x1 -> x0, waiting for transfers between devices: 24.1 us -> none  [shards(): lax.psum_scatter(lax.dot_general(out_weight, gated, (((0,), (1,)), ((), (...]
    all_to_all x2 -> x0, waiting for transfers between devices: 21.3 us -> none  [the longest x1 12.9 us: shards(): lax.all_to_all(product.T, 'ctx', split_axis=0, concat_axis=1, tiled=True)]
    pallas_call x0 -> x11, Pallas kernels: none -> 14.9 us  [the longest x2 4.4 us: shards(): pl.pallas_call(functools.partial(local_kernel, part, tail, height), in_sp...]
    ppermute x3 -> x8, waiting for transfers between devices: 1.17 us -> 10.2 us  [the longest x7 10.2 us: swap(): return lax.ppermute(value, axis, [(i, i ^ bits) for i in range(count)])]
    all_to_all x2 -> x0, starting transfers between devices: 8.86 us -> none  [the longest x1 5.08 us: shards(): lax.all_to_all(product.T, 'ctx', split_axis=0, concat_axis=1, tiled=True)]
    ppermute x3 -> x8, starting transfers between devices: 12.4 us -> 13.1 us  [the longest x7 8.16 us: swap(): return lax.ppermute(value, axis, [(i, i ^ bits) for i in range(count)])]
  transfers between devices with their start and end apart: 6 -> 8, of which waited for: 4 -> 3; matrix products, arithmetic and copies ran while one was open for 1% -> 0% of each run, Pallas kernels for 0% -> 25%
where the time goes in v2:
time: 39.4 us; the launch traced here: 39.1 us
  Pallas kernels  14.9 us (38%)
  starting transfers between devices  13.1 us (33%)
  waiting for transfers between devices  10.2 us (26%)
  other arithmetic  0.87 us (2%)
    ppermute x7, waiting for transfers between devices, swap(): return lax.ppermute(value, axis, [(i, i ^ bits) for i in range(count)])  10.2 us
    ppermute x7, starting transfers between devices, swap(): return lax.ppermute(value, axis, [(i, i ^ bits) for i in range(count)])  8.16 us
    ppermute x1, starting transfers between devices, shards(): halo = lax.ppermute(ends, 'ctx', [(i, i + 1) for i in range(count - 1)])  4.9 us
    pallas_call x2, Pallas kernels, shards(): pl.pallas_call(functools.partial(local_kernel, part, tail, height), in_sp...  4.4 us
    pallas_call x1, Pallas kernels, shards(): pl.pallas_call(functools.partial(state_kernel, tail, height), in_specs=[h...  3.39 us
    pallas_call x4, Pallas kernels, project(): pl.pallas_call(functools.partial(matmul_kernel, bits), in_specs=[here()]...  2.9 us
    pallas_call x1, Pallas kernels, shards(): pl.pallas_call(functools.partial(carry_kernel, height, stride, steps[-1])...  1.8 us
    pallas_call x1, Pallas kernels, shards(): pl.pallas_call(functools.partial(fetch_kernel, tail), in_specs=[far()] *...  1.52 us
  transfers between devices with their start and end apart: 8, of which 3 were waited for; matrix products, arithmetic and copies ran while one was open for 0% of the time, Pallas kernels for 25%

profile of v2, /device:TPU:0, one launch (start us, length us, event | category | flops | bytes accessed | tf_op | source)
XLA Modules:
  0.0 39.1 jit_solution(5890892651250430872)
XLA Ops:
  0.0 1.5 %shard_map.73 = (bf16[6,2048]{1,0:T(8,128)(2,1)S(1)}, bf16[128,2048]{1,0:T(8,128)(2,1)S(1)}, bf16[128,2048]{1,0:T(8,128)(2,1)S(1)}, bf16[128,2048]{1,0:T(8,128)(...) custom-call(bf16[128,2048]{1,0:T(8,128)(2,1)} %refs_0_.1, ...), custom_call_target="tpu_custom_call" | custom-call | tf_op jit(solution)/shard_map/pallas_call | solution.py:305
  1.5 4.9 %collective-permute-start = (bf16[6,2048]{1,0:T(8,128)(2,1)S(1)}, bf16[6,2048]{1,0:T(8,128)(2,1)S(1)}, u32[]{:S(2)}, u32[]{:S(2)}) collective-permute-start(bf16[6,2048]{1,0:T(8,128)(2,1)S(1)} %get-tuple-element.35), channel_id=1, source_target_pairs={{0,4},{4,8},{8,12},{12,16},{16,20},{20,24},{24,28},{1,5},{5,9},{9,... | collective-permute-start | bytes 73736 | tf_op jit(solution)/shard_map/ppermute | solution.py:314
  6.4 3.4 %shard_map.74 = (f32[2048,128]{1,0:T(8,128)S(1)}, f32[256,128]{1,0:T(8,128)S(1)}, f32[256,128]{1,0:T(8,128)S(1)}, f32[96,128]{1,0:T(8,128)S(1)}, bf16[1024,4096]{1,0:T(8,128)(2,1)S(1)}) custom-call(bf16[128,2048]{1,0:T(8,128)(2,1)S(1)} %get-tuple-element.30.k_ref, bf16[128,2048]{1,0:T(8,128)(2,1)S(1)} %get-tuple-element.31.v_ref, ...), custom_call_target="tpu_custom_call" | custom-call | flops 8388608 | bytes 8388608 | tf_op jit(solution)/shard_map/pallas_call | solution.py:316
  9.8 0.0 collective-permute-done.halo_ref
  9.8 0.1 shard_map.75
  9.9 1.6 %collective-permute-start.1 = (bf16[256,128]{1,0:T(8,128)(2,1)S(1)}, bf16[256,128]{1,0:T(8,128)(2,1)S(1)}, u32[]{:S(2)}, u32[]{:S(2)}) collective-permute-start(bf16[256,128]{1,0:T(8,128)(2,1)S(1)} %get-tuple-element.39), channel_id=1, source_target_pairs={{0,4},{4,0},{8,12},{12,8},{16,20},{20,16},{24,28},{28,24},{1,5},{5... | collective-permute-start | bytes 196616 | tf_op jit(solution)/shard_map/ppermute | solution.py:276
  11.5 2.7 %collective-permute-done.1.refs_0_ = bf16[256,128]{1,0:T(8,128)(2,1)S(1)} collective-permute-done((bf16[256,128]{1,0:T(8,128)(2,1)S(1)}, bf16[256,128]{1,0:T(8,128)(2,1)S(1)}, u32[]{:S(2)}, u32[]{:S(2)}) %collective-permute-start.1) | collective-permute-done | bytes 65568 | tf_op jit(solution)/shard_map/ppermute | solution.py:276
  14.3 0.8 %shard_map.76 = (f32[256,128]{1,0:T(8,128)}, bf16[256,128]{1,0:T(8,128)(2,1)S(1)}, f32[256,128]{1,0:T(8,128)S(1)}) custom-call(f32[256,128]{1,0:T(8,128)S(1)} %get-tuple-element.34.rate_ref, f32[256,128]{1,0:T(8,128)S(1)} %get-tuple-element.38.total_ref, f32[256,128]{1,0:T(8,128)S(1)} %broadcast_in_dim.3.before_ref, ...), custom_call_target="tpu_custom_call" | custom-call | tf_op jit(solution)/shard_map/pallas_call | solution.py:368
  15.0 1.6 %collective-permute-start.2 = (bf16[256,128]{1,0:T(8,128)(2,1)S(1)}, bf16[256,128]{1,0:T(8,128)(2,1)S(1)}, u32[]{:S(2)}, u32[]{:S(2)}) collective-permute-start(bf16[256,128]{1,0:T(8,128)(2,1)S(1)} %get-tuple-element.41), channel_id=1, source_target_pairs={{0,8},{4,12},{8,0},{12,4},{16,24},{20,28},{24,16},{28,20},{1,9},{5... | collective-permute-start | bytes 196616 | tf_op jit(solution)/shard_map/ppermute | solution.py:276
  16.6 2.6 %collective-permute-start.3 = (bf16[256,128]{1,0:T(8,128)(2,1)S(1)}, bf16[256,128]{1,0:T(8,128)(2,1)S(1)}, u32[]{:S(2)}, u32[]{:S(2)}) collective-permute-start(bf16[256,128]{1,0:T(8,128)(2,1)S(1)} %get-tuple-element.41), channel_id=1, source_target_pairs={{0,16},{4,20},{8,24},{12,28},{16,0},{20,4},{24,8},{28,12},{1,17},{... | collective-permute-start | bytes 196616 | tf_op jit(solution)/shard_map/ppermute | solution.py:276
  19.2 0.2 collective-permute-start.4
  19.4 2.2 %shard_map.78 = (f32[1024,128]{1,0:T(8,128)S(1)}, f32[1024,128]{1,0:T(8,128)S(1)}, f32[128,128]{1,0:T(8,128)S(1)}, bf16[512,4096]{1,0:T(8,128)(2,1)S(1)}) custom-call(bf16[6,2048]{1,0:T(8,128)(2,1)S(1)} %collective-permute-done.halo_ref, bf16[128,2048]{1,0:T(8,128)(2,1)S(1)} %get-tuple-element.42.q_ref, f32[3,3,2048]{2,1,0:T(4,128)S(1)} %get-tuple-element.32.taps_ref, ...), custom_call_target="tpu_custom_call" | custom-call | flops 8388608 | bytes 4194304 | tf_op jit(solution)/shard_map/pallas_call | solution.py:344
  21.6 2.2 %shard_map.77 = (f32[1024,128]{1,0:T(8,128)S(1)}, f32[1024,128]{1,0:T(8,128)S(1)}, f32[128,128]{1,0:T(8,128)S(1)}, bf16[512,4096]{1,0:T(8,128)(2,1)S(1)}) custom-call(bf16[6,2048]{1,0:T(8,128)(2,1)S(1)} %collective-permute-done.halo_ref, bf16[128,2048]{1,0:T(8,128)(2,1)S(1)} %get-tuple-element.42.q_ref, f32[3,3,2048]{2,1,0:T(4,128)S(1)} %get-tuple-element.32.taps_ref, ...), custom_call_target="tpu_custom_call" | custom-call | flops 8388608 | bytes 4194304 | tf_op jit(solution)/shard_map/pallas_call | solution.py:344
  23.8 0.0 collective-permute-done.2.refs_0_
  23.8 0.0 collective-permute-done.3.refs_1_
  23.9 1.4 %collective-permute-done.4.refs_2_ = bf16[256,128]{1,0:T(8,128)(2,1)S(1)} collective-permute-done((bf16[256,128]{1,0:T(8,128)(2,1)S(1)}, bf16[256,128]{1,0:T(8,128)(2,1)S(1)}, u32[]{:S(2)}, u32[]{:S(2)}) %collective-permute-start.4) | collective-permute-done | bytes 65568 | tf_op jit(solution)/shard_map/ppermute | solution.py:276
  25.3 1.8 %shard_map.79.gated_ref = bf16[128,2048]{1,0:T(8,128)(2,1)S(1)} custom-call(f32[256,128]{1,0:T(8,128)S(1)} %get-tuple-element.34.rate_ref, f32[256,128]{1,0:T(8,128)S(1)} %get-tuple-element.40.before_ref, bf16[256,128]{1,0:T(8,128)(2,1)S(1)} %collective-permute-done.2.refs_0_, bf16[256,128]{1,0:T(8,128)(2,1)S(1)} %collective-permute-done.3.refs_1_, ...), custom_call_target="tpu_custom_call" | custom-call | tf_op jit(solution)/shard_map/pallas_call | solution.py:377
  27.1 0.7 %shard_map.83 = bf16[128,1024]{1,0:T(8,128)(2,1)S(1)} custom-call(bf16[128,2048]{1,0:T(8,128)(2,1)S(1)} %shard_map.79.gated_ref, bf16[1024,4096]{1,0:T(8,128)(2,1)S(1)} %get-tuple-element.52.refs_0_, bf16[512,4096]{1,0:T(8,128)(2,1)S(1)} %get-tuple-element.53.refs_1_, bf16[512,4096]{1,0:T(8,128)(2,1)S(1)} %get-tuple-element.54.refs_2_), custom_call_target="tpu_custom_call" | custom-call | flops 536870912 | bytes 4194304 | tf_op jit(solution)/shard_map/pallas_call | solution.py:260
  27.8 0.1 collective-permute-start.6
  27.9 0.7 %shard_map.81 = bf16[128,1024]{1,0:T(8,128)(2,1)S(1)} custom-call(bf16[128,2048]{1,0:T(8,128)(2,1)S(1)} %shard_map.79.gated_ref, bf16[1024,4096]{1,0:T(8,128)(2,1)S(1)} %get-tuple-element.52.refs_0_, bf16[512,4096]{1,0:T(8,128)(2,1)S(1)} %get-tuple-element.53.refs_1_, bf16[512,4096]{1,0:T(8,128)(2,1)S(1)} %get-tuple-element.54.refs_2_), custom_call_target="tpu_custom_call" | custom-call | flops 536870912 | bytes 4194304 | tf_op jit(solution)/shard_map/pallas_call | solution.py:260
  28.6 0.6 %collective-permute-start.5 = (bf16[128,1024]{1,0:T(8,128)(2,1)S(1)}, bf16[128,1024]{1,0:T(8,128)(2,1)S(1)}, u32[]{:S(2)}, u32[]{:S(2)}) collective-permute-start(bf16[128,1024]{1,0:T(8,128)(2,1)S(1)} %shard_map.81), channel_id=1, source_target_pairs={{0,1},{1,0},{2,3},{3,2},{4,5},{5,4},{6,7},{7,6},{8,9},{9,8},{10,11... | collective-permute-start | bytes 786440 | tf_op jit(solution)/shard_map/ppermute | solution.py:276
  29.2 0.7 %shard_map.82 = f32[128,1024]{1,0:T(8,128)S(1)} custom-call(bf16[128,2048]{1,0:T(8,128)(2,1)S(1)} %shard_map.79.gated_ref, bf16[1024,4096]{1,0:T(8,128)(2,1)S(1)} %get-tuple-element.52.refs_0_, bf16[512,4096]{1,0:T(8,128)(2,1)S(1)} %get-tuple-element.53.refs_1_, bf16[512,4096]{1,0:T(8,128)(2,1)S(1)} %get-tuple-element.54.refs_2_), custom_call_target="tpu_custom_call" | custom-call | flops 536870912 | bytes 4194304 | tf_op jit(solution)/shard_map/pallas_call | solution.py:260
  29.9 0.0 collective-permute-done.6
  29.9 0.1 add_convert_fusion.1
  30.0 1.6 %collective-permute-start.7 = (bf16[128,1024]{1,0:T(8,128)(2,1)S(1)}, bf16[128,1024]{1,0:T(8,128)(2,1)S(1)}, u32[]{:S(2)}, u32[]{:S(2)}) collective-permute-start(bf16[128,1024]{1,0:T(8,128)(2,1)S(1)} %add_convert_fusion.1), channel_id=1, source_target_pairs={{0,2},{1,3},{2,0},{3,1},{4,6},{5,7},{6,4},{7,5},{8,10},{9,11},{10,... | collective-permute-start | bytes 786440 | tf_op jit(solution)/shard_map/ppermute | solution.py:276
  31.6 0.7 %shard_map.80 = f32[128,1024]{1,0:T(8,128)S(1)} custom-call(bf16[128,2048]{1,0:T(8,128)(2,1)S(1)} %shard_map.79.gated_ref, bf16[1024,4096]{1,0:T(8,128)(2,1)S(1)} %get-tuple-element.52.refs_0_, bf16[512,4096]{1,0:T(8,128)(2,1)S(1)} %get-tuple-element.53.refs_1_, bf16[512,4096]{1,0:T(8,128)(2,1)S(1)} %get-tuple-element.54.refs_2_), custom_call_target="tpu_custom_call" | custom-call | flops 536870912 | bytes 4194304 | tf_op jit(solution)/shard_map/pallas_call | solution.py:260
  32.3 0.0 collective-permute-done.5
  32.3 6.0 %collective-permute-done.7 = bf16[128,1024]{1,0:T(8,128)(2,1)S(1)} collective-permute-done((bf16[128,1024]{1,0:T(8,128)(2,1)S(1)}, bf16[128,1024]{1,0:T(8,128)(2,1)S(1)}, u32[]{:S(2)}, u32[]{:S(2)}) %collective-permute-start.7) | collective-permute-done | bytes 262176 | tf_op jit(solution)/shard_map/ppermute | solution.py:276
  38.3 0.8 %add_convert_fusion = bf16[128,1024]{1,0:T(8,128)(2,1)} fusion(bf16[128,1024]{1,0:T(8,128)(2,1)S(1)} %collective-permute-done.7, f32[128,1024]{1,0:T(8,128)S(1)} %shard_map.80, bf16[128,1024]{1,0:T(8,128)(2,1)S(1)} %collective-permute-done.5), kind=kLoop, calls=%fused_computation | loop fusion | flops 655360 | bytes 1310720 | tf_op jit(solution)/shard_map/convert_element_type | solution.py:404
  (1 shorter events, 0.0 us)
Async XLA Ops:
  1.5 8.3 %collective-permute-start = (bf16[6,2048]{1,0:T(8,128)(2,1)S(1)}, bf16[6,2048]{1,0:T(8,128)(2,1)S(1)}, u32[]{:S(2)}, u32[]{:S(2)}) collective-permute-start(bf16[6,2048]{1,0:T(8,128)(2,1)S(1)} %get-tuple-element.35), channel_id=1, source_target_pairs={{0,4},{4,8},{8,12},{12,16},{16,20},{20,24},{24,28},{1,5},{5,9},{9,... | collective-permute-start | bytes 73736 | tf_op jit(solution)/shard_map/ppermute | solution.py:314
  9.9 4.3 %collective-permute-start.1 = (bf16[256,128]{1,0:T(8,128)(2,1)S(1)}, bf16[256,128]{1,0:T(8,128)(2,1)S(1)}, u32[]{:S(2)}, u32[]{:S(2)}) collective-permute-start(bf16[256,128]{1,0:T(8,128)(2,1)S(1)} %get-tuple-element.39), channel_id=1, source_target_pairs={{0,4},{4,0},{8,12},{12,8},{16,20},{20,16},{24,28},{28,24},{1,5},{5... | collective-permute-start | bytes 196616 | tf_op jit(solution)/shard_map/ppermute | solution.py:276
  15.0 8.8 %collective-permute-start.2 = (bf16[256,128]{1,0:T(8,128)(2,1)S(1)}, bf16[256,128]{1,0:T(8,128)(2,1)S(1)}, u32[]{:S(2)}, u32[]{:S(2)}) collective-permute-start(bf16[256,128]{1,0:T(8,128)(2,1)S(1)} %get-tuple-element.41), channel_id=1, source_target_pairs={{0,8},{4,12},{8,0},{12,4},{16,24},{20,28},{24,16},{28,20},{1,9},{5... | collective-permute-start | bytes 196616 | tf_op jit(solution)/shard_map/ppermute | solution.py:276
  16.6 7.2 %collective-permute-start.3 = (bf16[256,128]{1,0:T(8,128)(2,1)S(1)}, bf16[256,128]{1,0:T(8,128)(2,1)S(1)}, u32[]{:S(2)}, u32[]{:S(2)}) collective-permute-start(bf16[256,128]{1,0:T(8,128)(2,1)S(1)} %get-tuple-element.41), channel_id=1, source_target_pairs={{0,16},{4,20},{8,24},{12,28},{16,0},{20,4},{24,8},{28,12},{1,17},{... | collective-permute-start | bytes 196616 | tf_op jit(solution)/shard_map/ppermute | solution.py:276
  19.2 6.1 %collective-permute-start.4 = (bf16[256,128]{1,0:T(8,128)(2,1)S(1)}, bf16[256,128]{1,0:T(8,128)(2,1)S(1)}, u32[]{:S(2)}, u32[]{:S(2)}) collective-permute-start(bf16[256,128]{1,0:T(8,128)(2,1)S(1)} %get-tuple-element.41), channel_id=1, source_target_pairs={{0,24},{4,28},{8,16},{12,20},{16,8},{20,12},{24,0},{28,4},{1,25},{... | collective-permute-start | bytes 196616 | tf_op jit(solution)/shard_map/ppermute | solution.py:276
  27.8 2.1 %collective-permute-start.6 = (bf16[128,1024]{1,0:T(8,128)(2,1)S(1)}, bf16[128,1024]{1,0:T(8,128)(2,1)S(1)}, u32[]{:S(2)}, u32[]{:S(2)}) collective-permute-start(bf16[128,1024]{1,0:T(8,128)(2,1)S(1)} %shard_map.83), channel_id=1, source_target_pairs={{0,1},{1,0},{2,3},{3,2},{4,5},{5,4},{6,7},{7,6},{8,9},{9,8},{10,11... | collective-permute-start | bytes 786440 | tf_op jit(solution)/shard_map/ppermute | solution.py:276
  28.6 3.7 %collective-permute-start.5 = (bf16[128,1024]{1,0:T(8,128)(2,1)S(1)}, bf16[128,1024]{1,0:T(8,128)(2,1)S(1)}, u32[]{:S(2)}, u32[]{:S(2)}) collective-permute-start(bf16[128,1024]{1,0:T(8,128)(2,1)S(1)} %shard_map.81), channel_id=1, source_target_pairs={{0,1},{1,0},{2,3},{3,2},{4,5},{5,4},{6,7},{7,6},{8,9},{9,8},{10,11... | collective-permute-start | bytes 786440 | tf_op jit(solution)/shard_map/ppermute | solution.py:276
  30.0 8.3 %collective-permute-start.7 = (bf16[128,1024]{1,0:T(8,128)(2,1)S(1)}, bf16[128,1024]{1,0:T(8,128)(2,1)S(1)}, u32[]{:S(2)}, u32[]{:S(2)}) collective-permute-start(bf16[128,1024]{1,0:T(8,128)(2,1)S(1)} %add_convert_fusion.1), channel_id=1, source_target_pairs={{0,2},{1,3},{2,0},{3,1},{4,6},{5,7},{6,4},{7,5},{8,10},{9,11},{10,... | collective-permute-start | bytes 786440 | tf_op jit(solution)/shard_map/ppermute | solution.py:276
